TPU v7x, 32 devices: a whole 2x2x4 slice. The times are simulated.
32 devices in a mesh: dp: 8 (over z, core), expert: 4 (over y, x).
Axes of the slice: x: 2, y: 2, z: 4, core: 2. Of those that a mesh axis runs over, the one named last changes fastest.
Arguments:
- tokens: bfloat16 [24576, 2048], P(('dp', 'expert')), may hold values from -6 to 6
- target: bfloat16 [24576, 2048], P(('dp', 'expert')), may hold values from -4 to 4
- route_index: int32 [8, 4, 4, 16], P('dp', None, 'expert'), may hold values from 0 to 767, as said below
- route_count: int32 [8, 4, 4], P('dp', None, 'expert'), may hold values from 1 to 16, as said below
- route_gate: float32 [8, 4, 4, 16], P('dp', None, 'expert'), may hold values from 0.1 to 1
- gate_weight: bfloat16 [2048, 4, 768], P('dp', 'expert'), may hold values from -0.125 to 0.125
- up_weight: bfloat16 [2048, 4, 768], P('dp', 'expert'), may hold values from -0.125 to 0.125
- down_weight: bfloat16 [2048, 4, 768], P('dp', 'expert'), may hold values from -0.21875 to 0.21875
Outputs:
- token_grad: bfloat16 [24576, 2048], P(('dp', 'expert'))
- gate_gradient: float32 [2048, 4, 768], P('dp', 'expert')
- up_gradient: float32 [2048, 4, 768], P('dp', 'expert')
- down_gradient: float32 [2048, 4, 768], P('dp', 'expert')
Inputs may be any that keep to these rules, and one draw needn't show every extreme that they name: `route_index`: within each list of 16 slots the indices are distinct; each names a token of the source device. `route_count`: in every group one expert has all 16 slots live from every source device; slots at or beyond the count are unused.
All inputs are finite; a program needn't handle non-finite values.
Results may differ from a plain program's by a relative error of at most 0.0059.
Values may be sent and summed in bfloat16 or wider, within the bound.
A program may use at most 128 MiB of HBM per device.

v0:
```python
import jax
import jax.numpy as jnp
from jax import lax
from jax.sharding import PartitionSpec as P


def to_owners(block):
    return lax.all_to_all(block, "expert", split_axis=0, concat_axis=1, tiled=True)


def to_sources(block):
    return lax.all_to_all(block, "expert", split_axis=1, concat_axis=0, tiled=True)


def on_device(
    tokens, target, route_index, route_count, route_gate, gate_weight, up_weight, down_weight
):
    groups = lax.axis_size("dp")
    sources = lax.axis_size("expert")
    local_index = route_index[0, :, 0, :]
    live_count = route_count[0, :, 0]
    per_source = local_index.shape[1]
    model_width = tokens.shape[1]
    usable = jnp.arange(per_source, dtype=jnp.int32)[None, :] < live_count[:, None]
    slot_weight = jnp.where(usable, route_gate[0, :, 0, :], 0.0)
    outgoing = tokens[local_index] * usable[:, :, None].astype(tokens.dtype)
    expert_rows = to_owners(outgoing)
    full_gate, full_up, full_down = (
        lax.all_gather(gate_weight, "dp", axis=0, tiled=True),
        lax.all_gather(up_weight, "dp", axis=0, tiled=True),
        lax.all_gather(down_weight, "dp", axis=0, tiled=True),
    )
    gate_pre = jnp.einsum(
        "erd,def->erf", expert_rows, full_gate, preferred_element_type=jnp.float32
    )
    up_pre = jnp.einsum("erd,def->erf", expert_rows, full_up, preferred_element_type=jnp.float32)
    sigma = jax.nn.sigmoid(gate_pre)
    active = gate_pre * sigma
    hidden = (active * up_pre).astype(jnp.bfloat16)
    expert_out = jnp.einsum(
        "erf,def->erd", hidden, full_down, preferred_element_type=jnp.float32
    ).astype(jnp.bfloat16)
    returned = to_sources(expert_out)
    flat_index = local_index.reshape(-1)
    combined = (
        jnp.zeros((tokens.shape[0], model_width), jnp.float32)
        .at[flat_index]
        .add((slot_weight[:, :, None] * returned.astype(jnp.float32)).reshape(-1, model_width))
    )
    out_grad = combined - target.astype(jnp.float32)
    slot_grad = (slot_weight[:, :, None] * out_grad[local_index]).astype(jnp.bfloat16)
    owner_grad = to_owners(slot_grad)
    hidden_grad = jnp.einsum(
        "erd,def->erf", owner_grad, full_down, preferred_element_type=jnp.float32
    )
    gate_grad = (hidden_grad * up_pre * sigma * (1.0 + gate_pre * (1.0 - sigma))).astype(
        jnp.bfloat16
    )
    up_grad = (hidden_grad * active).astype(jnp.bfloat16)
    row_grad = (
        jnp.einsum("erf,def->erd", gate_grad, full_gate, preferred_element_type=jnp.float32)
        + jnp.einsum("erf,def->erd", up_grad, full_up, preferred_element_type=jnp.float32)
    ).astype(jnp.bfloat16)
    came_back = to_sources(row_grad)
    token_grad = (
        jnp.zeros((tokens.shape[0], model_width), jnp.float32)
        .at[flat_index]
        .add(came_back.astype(jnp.float32).reshape(-1, model_width))
        .astype(jnp.bfloat16)
    )
    factor = (groups * sources * per_source) ** (-0.5)
    rows_every, grad_every = (
        lax.all_to_all(expert_rows, "dp", split_axis=2, concat_axis=1, tiled=True),
        lax.all_to_all(owner_grad, "dp", split_axis=2, concat_axis=1, tiled=True),
    )
    hidden_piece = lax.all_gather(hidden, "dp", axis=1, tiled=True)
    gate_piece = lax.all_gather(gate_grad, "dp", axis=1, tiled=True)
    up_piece = lax.all_gather(up_grad, "dp", axis=1, tiled=True)
    gate_sum = jnp.einsum(
        "erd,erf->def", rows_every, gate_piece, preferred_element_type=jnp.float32
    )
    up_sum = jnp.einsum("erd,erf->def", rows_every, up_piece, preferred_element_type=jnp.float32)
    down_sum = jnp.einsum(
        "erd,erf->def", grad_every, hidden_piece, preferred_element_type=jnp.float32
    )
    gate_gradient = gate_sum * factor
    up_gradient = up_sum * factor
    down_gradient = down_sum * factor
    return (token_grad, gate_gradient, up_gradient, down_gradient)


def solution(mesh):
    return jax.shard_map(
        on_device,
        mesh=mesh,
        in_specs=(
            P(("dp", "expert"), None),
            P(("dp", "expert"), None),
            P("dp", None, "expert", None),
            P("dp", None, "expert"),
            P("dp", None, "expert", None),
            P("dp", "expert", None),
            P("dp", "expert", None),
            P("dp", "expert", None),
        ),
        out_specs=(
            P(("dp", "expert"), None),
            P("dp", "expert", None),
            P("dp", "expert", None),
            P("dp", "expert", None),
        ),
        check_vma=False,
    )
```

profile of v0, /device:TPU:0, one launch (start us, length us, event | category | flops | bytes accessed | tf_op | source)
XLA Modules:
  0.0 305.2 jit_solution(9919206521907058066)
XLA Ops:
  11.8 5.2 %all-to-all-start = ((bf16[4,16,2048]{2,1,0:T(8,128)(2,1)}), bf16[4,16,2048]{2,1,0:T(8,128)(2,1)S(1)}, u32[]{:S(2)}, u32[]{:S(2)}) async-start(bf16[4,16,2048]{2,1,0:T(8,128)(2,1)} %broadcast_multiply_fusion), calls=%async_computation | async-start | bytes 524288 | tf_op jit(solution)/shard_map/all_to_all | solution.py:8
  18.3 4.1 %all-to-all-done = bf16[4,16,2048]{2,1,0:T(8,128)(2,1)S(1)} async-done(((bf16[4,16,2048]{2,1,0:T(8,128)(2,1)}), bf16[4,16,2048]{2,1,0:T(8,128)(2,1)S(1)}, u32[]{:S(2)}, u32[]{:S(2)}) %all-to-all-start) | async-done | bytes 262176 | tf_op jit(solution)/shard_map/all_to_all | solution.py:8
  24.9 13.3 %reduce.10 = bf16[2048,64]{1,0:T(8,128)(2,1)} reduce(bf16[2048,1,64]{2,1,0:T(2,128)(2,1)} %bitcast.114, bf16[]{:T(256)} %broadcast.134), dimensions={1}, to_apply=%bitcast.86.reduce_sub_computation | reduce | bytes 524290
  40.3 4.9 %all-to-all-start.4 = ((bf16[8,2,8192]{2,1,0:T(2,128)(2,1)}), bf16[8,2,8192]{2,1,0:T(2,128)(2,1)}, u32[]{:S(2)}, u32[]{:S(2)}) async-start(bf16[8,2,8192]{2,1,0:T(2,128)(2,1)} %reshape.301), calls=%async_computation.4 | async-start | bytes 524288 | tf_op jit(solution)/shard_map/all_to_all | solution.py:73
  46.6 8.4 %all-to-all-done.4 = bf16[8,2,8192]{2,1,0:T(2,128)(2,1)} async-done(((bf16[8,2,8192]{2,1,0:T(2,128)(2,1)}), bf16[8,2,8192]{2,1,0:T(2,128)(2,1)}, u32[]{:S(2)}, u32[]{:S(2)}) %all-to-all-start.4) | async-done | bytes 262176 | tf_op jit(solution)/shard_map/all_to_all | solution.py:73
  58.4 3.4 %copy.41 = bf16[1,64,2048]{2,1,0:T(8,128)(2,1)} copy(bf16[1,64,2048]{1,0,2:T(2,128)(2,1)} %bitcast.112) | data formatting | bytes 524288 | tf_op jit(solution)/shard_map/all_to_all | solution.py:73
  66.8 24.2 %all-gather.9.cloned.1.call-done = bf16[2048,1,768]{2,0,1:T(8,128)(2,1)} async-done(((bf16[256,1,768]{2,0,1:T(8,128)(2,1)}), bf16[2048,1,768]{2,0,1:T(8,128)(2,1)}) %all-gather.9.cloned.1.call-update) | async-done | bytes 3145744 | tf_op jit(solution)/shard_map/all_gather | solution.py:30
  94.1 35.6 %all-gather.11.cloned.1.call-done = bf16[2048,1,768]{2,0,1:T(8,128)(2,1)} async-done(((bf16[256,1,768]{2,0,1:T(8,128)(2,1)}), bf16[2048,1,768]{2,0,1:T(8,128)(2,1)}) %all-gather.11.cloned.1.call-update) | async-done | bytes 3145744 | tf_op jit(solution)/shard_map/all_gather | solution.py:31
  133.9 3.8 %reduce.8 = bf16[64,2048]{1,0:T(8,128)(2,1)} reduce(bf16[64,1,2048]{2,1,0:T(2,128)(2,1)} %bitcast.123, bf16[]{:T(256)} %broadcast.134), dimensions={1}, to_apply=%bitcast.109.reduce_sub_computation | reduce | bytes 524290
  139.5 4.2 %all-to-all-start.1 = ((bf16[4,2,16384]{2,1,0:T(2,128)(2,1)}), bf16[4,2,16384]{2,1,0:T(2,128)(2,1)}, u32[]{:S(2)}, u32[]{:S(2)}) async-start(bf16[4,2,16384]{2,1,0:T(2,128)(2,1)} %reshape.297), calls=%async_computation.1 | async-start | bytes 524288 | tf_op jit(solution)/shard_map/all_to_all | solution.py:12
  143.8 5.8 %all-to-all-done.1 = bf16[4,2,16384]{2,1,0:T(2,128)(2,1)} async-done(((bf16[4,2,16384]{2,1,0:T(2,128)(2,1)}), bf16[4,2,16384]{2,1,0:T(2,128)(2,1)}, u32[]{:S(2)}, u32[]{:S(2)}) %all-to-all-start.1) | async-done | bytes 262176 | tf_op jit(solution)/shard_map/all_to_all | solution.py:12
  151.5 5.1 %scatter_custom_fusion = f32[768,2048]{1,0:T(8,128)} fusion(s32[64]{0:T(128)S(1)} %fusion.41, f32[]{:T(128)} %constant.5.clone.1, bf16[1,64,2048]{2,0,1:T(2,128)(2,1)} %bitcast.122, f32[64]{0:T(128)S(1)} %broadcast_select_fusion.1), kind=kCustom, calls=%fused_computation.19 | custom fusion | flops 393216 | bytes 6554116 | tf_op jit(solution)/shard_map/scatter-add | solution.py:48
  156.6 7.9 %convert_subtract_fusion = f32[768,2048]{1,0:T(8,128)} fusion(f32[768,2048]{1,0:T(8,128)} %scatter_custom_fusion, bf16[768,2048]{1,0:T(8,128)(2,1)} %param.9), kind=kLoop, calls=%fused_computation.4 | loop fusion | flops 3145728 | bytes 15728640 | tf_op jit(solution)/shard_map/sub | solution.py:50
  164.4 4.6 %gather_fusion.1 = f32[64,2048]{1,0:T(8,128)} fusion(f32[768,2048]{1,0:T(8,128)} %convert_subtract_fusion, s32[1024]{0:T(1024)S(1)} %pad_clamp_fusion), kind=kCustom, calls=%fused_computation.1 | custom fusion | bytes 1048832 | tf_op jit(solution)/shard_map/gather | solution.py:51
  170.8 4.1 %all-to-all-start.2 = ((bf16[4,16,2048]{2,1,0:T(8,128)(2,1)}), bf16[4,16,2048]{2,1,0:T(8,128)(2,1)}, u32[]{:S(2)}, u32[]{:S(2)}) async-start(bf16[4,16,2048]{2,1,0:T(8,128)(2,1)} %multiply_convert_fusion), calls=%async_computation.2 | async-start | bytes 524288 | tf_op jit(solution)/shard_map/all_to_all | solution.py:8
  174.9 16.5 %all-gather.2 = bf16[512,768]{1,0:T(8,128)(2,1)} all-gather(bf16[64,768]{1,0:T(8,128)(2,1)S(1)} %get-tuple-element.28), channel_id=4, replica_groups=mesh['dp'=8,'expert'=4] {'dp'}, dimensions={0}, use_global_device_ids=true | all-gather | bytes 884736 | tf_op jit(solution)/shard_map/all_gather | solution.py:76
  197.7 3.8 %reduce.9 = bf16[64,2048]{1,0:T(8,128)(2,1)} reduce(bf16[64,1,2048]{2,1,0:T(2,128)(2,1)} %bitcast.124, bf16[]{:T(256)} %broadcast.134), dimensions={1}, to_apply=%bitcast.108.reduce_sub_computation | reduce | bytes 524290
  203.4 4.2 %all-to-all-start.3 = ((bf16[4,2,16384]{2,1,0:T(2,128)(2,1)}), bf16[4,2,16384]{2,1,0:T(2,128)(2,1)}, u32[]{:S(2)}, u32[]{:S(2)}) async-start(bf16[4,2,16384]{2,1,0:T(2,128)(2,1)} %reshape.299), calls=%async_computation.3 | async-start | bytes 524288 | tf_op jit(solution)/shard_map/all_to_all | solution.py:12
  207.6 16.5 %all-gather = bf16[512,768]{1,0:T(8,128)(2,1)S(1)} all-gather(bf16[64,768]{1,0:T(8,128)(2,1)} %copy-done.4), channel_id=2, replica_groups=mesh['dp'=8,'expert'=4] {'dp'}, dimensions={0}, use_global_device_ids=true | all-gather | bytes 884736 | tf_op jit(solution)/shard_map/all_gather | solution.py:77
  231.8 13.3 %reduce.11 = bf16[2048,64]{1,0:T(8,128)(2,1)} reduce(bf16[2048,1,64]{2,1,0:T(2,128)(2,1)} %bitcast.115, bf16[]{:T(256)} %broadcast.134), dimensions={1}, to_apply=%bitcast.88.reduce_sub_computation | reduce | bytes 524290
  247.3 4.1 %all-to-all-start.5 = ((bf16[8,2,8192]{2,1,0:T(2,128)(2,1)}), bf16[8,2,8192]{2,1,0:T(2,128)(2,1)}, u32[]{:S(2)}, u32[]{:S(2)}) async-start(bf16[8,2,8192]{2,1,0:T(2,128)(2,1)} %reshape.303), calls=%async_computation.5 | async-start | bytes 524288 | tf_op jit(solution)/shard_map/all_to_all | solution.py:74
  251.3 19.9 %all-gather.1 = bf16[512,768]{1,0:T(8,128)(2,1)S(1)} all-gather(bf16[64,768]{1,0:T(8,128)(2,1)S(1)} %get-tuple-element.25), channel_id=3, replica_groups=mesh['dp'=8,'expert'=4] {'dp'}, dimensions={0}, use_global_device_ids=true | all-gather | bytes 884736 | tf_op jit(solution)/shard_map/all_gather | solution.py:78
  277.5 5.1 %scatter_custom_fusion.1 = f32[768,2048]{1,0:T(8,128)} fusion(s32[64]{0:T(128)S(1)} %fusion.41, f32[]{:T(128)} %constant.5.clone.1, bf16[1,64,2048]{2,0,1:T(2,128)(2,1)} %bitcast.125), kind=kCustom, calls=%fused_computation.17 | custom fusion | flops 262144 | bytes 6553604 | tf_op jit(solution)/shard_map/scatter-add | solution.py:68
  282.5 4.9 %convert_element_type.75 = bf16[768,2048]{1,0:T(8,128)(2,1)} convert(f32[768,2048]{1,0:T(8,128)} %scatter_custom_fusion.1) | non-fusion elementwise | flops 1572864 | bytes 9437184 | tf_op jit(solution)/shard_map/convert_element_type | solution.py:69
  (75 shorter events, 68.6 us)
Async XLA Ops:
  7.2 3.0 copy-start
  7.2 10.4 %copy-start.5 = (s32[1,4,1,16]{3,2,1,0:T(1,128)S(1)}, s32[1,4,1,16]{3,2,1,0:T(1,128)}, u32[]{:S(2)}) copy-start(s32[1,4,1,16]{3,2,1,0:T(1,128)} %param.10) | copy-start | bytes 772
  7.2 3.8 %copy-start.7 = (s32[1,4,1]{1,2,0:T(1,128)S(1)}, s32[1,4,1]{1,2,0:T(1,128)}, u32[]{:S(2)}) copy-start(s32[1,4,1]{1,2,0:T(1,128)} %param.11) | copy-start | bytes 52
  7.2 56.3 %all-gather.7.cloned.1.call-start = ((), (), s32[]{:S(2)}) async-start(), calls=%async_computation.6 | async-start | bytes 3538944 | tf_op jit(solution)/shard_map/all_gather | solution.py:29
  7.9 83.0 %all-gather.9.cloned.1.call-start = ((), (), s32[]{:S(2)}) async-start(), calls=%async_computation.7 | async-start | bytes 3538944 | tf_op jit(solution)/shard_map/all_gather | solution.py:30
  8.7 121.0 %all-gather.11.cloned.1.call-start = ((), (), s32[]{:S(2)}) async-start(), calls=%async_computation.8 | async-start | bytes 3538944 | tf_op jit(solution)/shard_map/all_gather | solution.py:31
  10.9 34.9 %copy-start.6 = (f32[1,4,1,16]{3,2,1,0:T(1,128)S(1)}, f32[1,4,1,16]{3,2,1,0:T(1,128)}, u32[]{:S(2)}) copy-start(f32[1,4,1,16]{3,2,1,0:T(1,128)} %param.12) | copy-start | bytes 772
  11.8 10.6 %all-to-all-start = ((bf16[4,16,2048]{2,1,0:T(8,128)(2,1)}), bf16[4,16,2048]{2,1,0:T(8,128)(2,1)S(1)}, u32[]{:S(2)}, u32[]{:S(2)}) async-start(bf16[4,16,2048]{2,1,0:T(8,128)(2,1)} %broadcast_multiply_fusion), calls=%async_computation | async-start | bytes 524288 | tf_op jit(solution)/shard_map/all_to_all | solution.py:8
  40.3 14.7 %all-to-all-start.4 = ((bf16[8,2,8192]{2,1,0:T(2,128)(2,1)}), bf16[8,2,8192]{2,1,0:T(2,128)(2,1)}, u32[]{:S(2)}, u32[]{:S(2)}) async-start(bf16[8,2,8192]{2,1,0:T(2,128)(2,1)} %reshape.301), calls=%async_computation.4 | async-start | bytes 524288 | tf_op jit(solution)/shard_map/all_to_all | solution.py:73
  94.1 49.6 %copy-start.3 = (bf16[8,8,8,256]{3,2,1,0:T(8,128)(2,1)S(1)}, bf16[8,8,8,256]{3,2,1,0:T(8,128)(2,1)}, u32[]{:S(2)}) copy-start(bf16[8,8,8,256]{3,2,1,0:T(8,128)(2,1)} %copy.49) | copy-start | bytes 786436
  139.5 10.2 %all-to-all-start.1 = ((bf16[4,2,16384]{2,1,0:T(2,128)(2,1)}), bf16[4,2,16384]{2,1,0:T(2,128)(2,1)}, u32[]{:S(2)}, u32[]{:S(2)}) async-start(bf16[4,2,16384]{2,1,0:T(2,128)(2,1)} %reshape.297), calls=%async_computation.1 | async-start | bytes 524288 | tf_op jit(solution)/shard_map/all_to_all | solution.py:12
  170.8 20.5 %all-to-all-start.2 = ((bf16[4,16,2048]{2,1,0:T(8,128)(2,1)}), bf16[4,16,2048]{2,1,0:T(8,128)(2,1)}, u32[]{:S(2)}, u32[]{:S(2)}) async-start(bf16[4,16,2048]{2,1,0:T(8,128)(2,1)} %multiply_convert_fusion), calls=%async_computation.2 | async-start | bytes 524288 | tf_op jit(solution)/shard_map/all_to_all | solution.py:8
  191.4 3.0 copy-start.2
  191.4 4.1 %copy-start.1 = (bf16[2048,1,768]{2,0,1:T(8,128)(2,1)S(1)}, bf16[2048,1,768]{2,0,1:T(8,128)(2,1)}, u32[]{:S(2)}) copy-start(bf16[2048,1,768]{2,0,1:T(8,128)(2,1)} %all-gather.7.cloned.1.call-done) | copy-start | bytes 9437188
  194.2 2.3 copy-start.4
  203.4 43.9 %all-to-all-start.3 = ((bf16[4,2,16384]{2,1,0:T(2,128)(2,1)}), bf16[4,2,16384]{2,1,0:T(2,128)(2,1)}, u32[]{:S(2)}, u32[]{:S(2)}) async-start(bf16[4,2,16384]{2,1,0:T(2,128)(2,1)} %reshape.299), calls=%async_computation.3 | async-start | bytes 524288 | tf_op jit(solution)/shard_map/all_to_all | solution.py:12
  247.3 40.2 %all-to-all-start.5 = ((bf16[8,2,8192]{2,1,0:T(2,128)(2,1)}), bf16[8,2,8192]{2,1,0:T(2,128)(2,1)}, u32[]{:S(2)}, u32[]{:S(2)}) async-start(bf16[8,2,8192]{2,1,0:T(2,128)(2,1)} %reshape.303), calls=%async_computation.5 | async-start | bytes 524288 | tf_op jit(solution)/shard_map/all_to_all | solution.py:74
Sparse Core Ops, SparseCore 0:
  9.6 40.9 all-gather.6
  52.3 38.6 all-gather.8
  92.6 37.1 all-gather.10
where the time goes:
time: 307 us; the launch traced here: 305 us
  waiting for transfers between devices  80.1 us (26%)
  other arithmetic  62 us (20%)
  blocking collectives  52.9 us (17%)
  local copies, waits for them, and re-layouts  50.3 us (16%)
  starting transfers between devices  26.7 us (9%)
  matrix products  19.3 us (6%)
  between operations  13.9 us (5%)
    all_gather x1, waiting for transfers between devices, on_device(): lax.all_gather(down_weight, 'dp', axis=0, tiled=True)  35.6 us
    unnamed x6, other arithmetic  35.6 us
    unnamed x32, local copies, waits for them, and re-layouts  31.1 us
    all_gather x1, waiting for transfers between devices, on_device(): lax.all_gather(up_weight, 'dp', axis=0, tiled=True)  24.2 us
    all_gather x1, blocking collectives, on_device(): up_piece = lax.all_gather(up_grad, 'dp', axis=1, tiled=True)  19.9 us
    all_gather x1, blocking collectives, on_device(): gate_piece = lax.all_gather(gate_grad, 'dp', axis=1, tiled=True)  16.5 us
    all_gather x1, blocking collectives, on_device(): hidden_piece = lax.all_gather(hidden, 'dp', axis=1, tiled=True)  16.5 us
    all_to_all x2, starting transfers between devices, to_owners(): lax.all_to_all(block, 'expert', split_axis=0, concat_axis=1, tiled=True)  9.24 us
  transfers between devices with their start and end apart: 9, of which 5 were waited for; matrix products, arithmetic and copies ran while one was open for 25% of the time, Pallas kernels for 0%

commit v1 on v0

--- a/solution.py
+++ b/solution.py
@@ -2,6 +2,17 @@
 import jax.numpy as jnp
 from jax import lax
 from jax.sharding import PartitionSpec as P
+from jax.lax import axis_index, axis_size, ppermute
+
+
+def carry_steps_all_here(obj, device_axis):
+    series = [obj]
+    n_parts = axis_size(device_axis)
+    for c in range(n_parts - 1):
+        then = ppermute(series[-1], device_axis, [(d, (d + 1) % n_parts) for d in range(n_parts)])
+        series.append(then)
+    state_now = jnp.concatenate(series[::-1], 1)
+    return jnp.roll(state_now, (axis_index(device_axis) + 1) * obj.shape[1], 1)
 
 
 def to_owners(block):
@@ -75,7 +86,7 @@
     )
     hidden_piece = lax.all_gather(hidden, "dp", axis=1, tiled=True)
     gate_piece = lax.all_gather(gate_grad, "dp", axis=1, tiled=True)
-    up_piece = lax.all_gather(up_grad, "dp", axis=1, tiled=True)
+    up_piece = carry_steps_all_here(up_grad, "dp")
     gate_sum = jnp.einsum(
         "erd,erf->def", rows_every, gate_piece, preferred_element_type=jnp.float32
     )

time: 307 us -> 326 us (1.062)
  waiting for transfers between devices: 80.1 us -> 102 us
  blocking collectives: 52.9 us -> 37.6 us
  local copies, waits for them, and re-layouts: 50.3 us -> 63.1 us
    all_gather x1 -> x0, blocking collectives: 19.9 us -> none  [on_device(): up_piece = lax.all_gather(up_grad, 'dp', axis=1, tiled=True)]
    all_gather x1, waiting for transfers between devices: 24.2 us -> 37.2 us  [on_device(): lax.all_gather(up_weight, 'dp', axis=0, tiled=True)]
    ppermute x0 -> x7, waiting for transfers between devices: none -> 12.7 us  [carry_steps_all_here(): ppermute(series[-1], device_axis, [(d, (d + 1) % n_parts) for d in range(...]
    unnamed x32 -> x51, local copies, waits for them, and re-layouts: 31.1 us -> 42.7 us
    all_to_all x1, waiting for transfers between devices: 8.38 us -> 0.01 us  [on_device(): lax.all_to_all(expert_rows, 'dp', split_axis=2, concat_axis=1, tiled=True)]
    all_to_all x2, waiting for transfers between devices: 5.82 us -> 0.01 us  [to_sources(): lax.all_to_all(block, 'expert', split_axis=1, concat_axis=0, tiled=True)]
    all_gather x1, waiting for transfers between devices: 0.01 us -> 5.51 us  [on_device(): lax.all_gather(gate_weight, 'dp', axis=0, tiled=True)]
    all_to_all x2, waiting for transfers between devices: 4.11 us -> 8.51 us  [to_owners(): lax.all_to_all(block, 'expert', split_axis=0, concat_axis=1, tiled=True)]
  transfers between devices with their start and end apart: 9 -> 16, of which waited for: 5 -> 8; matrix products, arithmetic and copies ran while one was open for 25% -> 32% of each run, Pallas kernels for 0% -> 0%
where the time goes in v1:
time: 326 us; the launch traced here: 323 us
  waiting for transfers between devices  102 us (31%)
  local copies, waits for them, and re-layouts  63.1 us (19%)
  other arithmetic  61 us (19%)
  blocking collectives  37.6 us (12%)
  starting transfers between devices  27.6 us (8%)
  matrix products  18.2 us (6%)
  between operations  14 us (4%)
    unnamed x51, local copies, waits for them, and re-layouts  42.7 us
    all_gather x1, waiting for transfers between devices, on_device(): lax.all_gather(up_weight, 'dp', axis=0, tiled=True)  37.2 us
    all_gather x1, waiting for transfers between devices, on_device(): lax.all_gather(down_weight, 'dp', axis=0, tiled=True)  35.6 us
    unnamed x6, other arithmetic  34.6 us
    all_gather x1, blocking collectives, on_device(): gate_piece = lax.all_gather(gate_grad, 'dp', axis=1, tiled=True)  20 us
    all_gather x1, blocking collectives, on_device(): hidden_piece = lax.all_gather(hidden, 'dp', axis=1, tiled=True)  17.6 us
    ppermute x7, waiting for transfers between devices, carry_steps_all_here(): ppermute(series[-1], device_axis, [(d, (d + 1) % n_parts) for d in range(...  12.7 us
    all_to_all x2, starting transfers between devices, to_owners(): lax.all_to_all(block, 'expert', split_axis=0, concat_axis=1, tiled=True)  9.38 us
  transfers between devices with their start and end apart: 16, of which 8 were waited for; matrix products, arithmetic and copies ran while one was open for 32% of the time, Pallas kernels for 0%

profile of v1, /device:TPU:0, one launch (start us, length us, event | category | flops | bytes accessed | tf_op | source)
XLA Modules:
  0.0 323.1 jit_solution(6411702034247937369)
XLA Ops:
  11.8 5.2 %all-to-all-start = ((bf16[4,16,2048]{2,1,0:T(8,128)(2,1)}), bf16[4,16,2048]{2,1,0:T(8,128)(2,1)S(1)}, u32[]{:S(2)}, u32[]{:S(2)}) async-start(bf16[4,16,2048]{2,1,0:T(8,128)(2,1)} %broadcast_multiply_fusion), calls=%async_computation | async-start | bytes 524288 | tf_op jit(solution)/shard_map/all_to_all | solution.py:19
  24.8 13.3 %reduce.10 = bf16[2048,64]{1,0:T(8,128)(2,1)} reduce(bf16[2048,1,64]{2,1,0:T(2,128)(2,1)} %bitcast.119, bf16[]{:T(256)} %broadcast.135), dimensions={1}, to_apply=%bitcast.92.reduce_sub_computation | reduce | bytes 524290
  40.2 4.9 %all-to-all-start.4 = ((bf16[8,2,8192]{2,1,0:T(2,128)(2,1)}), bf16[8,2,8192]{2,1,0:T(2,128)(2,1)}, u32[]{:S(2)}, u32[]{:S(2)}) async-start(bf16[8,2,8192]{2,1,0:T(2,128)(2,1)} %reshape.299), calls=%async_computation.4 | async-start | bytes 524288 | tf_op jit(solution)/shard_map/all_to_all | solution.py:84
  45.1 5.5 %all-gather.6.cloned.1.call-done = bf16[2048,1,768]{2,0,1:T(8,128)(2,1)} async-done(((bf16[256,1,768]{2,0,1:T(8,128)(2,1)}), bf16[2048,1,768]{2,0,1:T(8,128)(2,1)}) %all-gather.6.cloned.1.call-update) | async-done | bytes 3145744 | tf_op jit(solution)/shard_map/all_gather | solution.py:40
  53.8 37.2 %all-gather.8.cloned.1.call-done = bf16[2048,1,768]{2,0,1:T(8,128)(2,1)} async-done(((bf16[256,1,768]{2,0,1:T(8,128)(2,1)}), bf16[2048,1,768]{2,0,1:T(8,128)(2,1)}) %all-gather.8.cloned.1.call-update) | async-done | bytes 3145744 | tf_op jit(solution)/shard_map/all_gather | solution.py:41
  94.2 35.6 %all-gather.10.cloned.1.call-done = bf16[2048,1,768]{2,0,1:T(8,128)(2,1)} async-done(((bf16[256,1,768]{2,0,1:T(8,128)(2,1)}), bf16[2048,1,768]{2,0,1:T(8,128)(2,1)}) %all-gather.10.cloned.1.call-update) | async-done | bytes 3145744 | tf_op jit(solution)/shard_map/all_gather | solution.py:42
  137.9 3.6 %all-to-all-start.1 = ((bf16[4,2,16384]{2,1,0:T(2,128)(2,1)}), bf16[4,2,16384]{2,1,0:T(2,128)(2,1)S(1)}, u32[]{:S(2)}, u32[]{:S(2)}) async-start(bf16[4,2,16384]{2,1,0:T(2,128)(2,1)} %reshape.295), calls=%async_computation.1 | async-start | bytes 524288 | tf_op jit(solution)/shard_map/all_to_all | solution.py:23
  145.0 3.4 %copy.41 = bf16[1,64,2048]{2,1,0:T(8,128)(2,1)} copy(bf16[1,64,2048]{1,0,2:T(2,128)(2,1)} %bitcast.117) | data formatting | bytes 524288 | tf_op jit(solution)/shard_map/all_to_all | solution.py:84
  151.0 5.1 %scatter_custom_fusion = f32[768,2048]{1,0:T(8,128)} fusion(s32[64]{0:T(128)S(1)} %fusion.43, f32[]{:T(128)} %constant.15.clone.1, bf16[1,64,2048]{2,0,1:T(2,128)(2,1)} %bitcast.127, f32[64]{0:T(128)S(1)} %broadcast_select_fusion.1), kind=kCustom, calls=%fused_computation.19 | custom fusion | flops 393216 | bytes 6554116 | tf_op jit(solution)/shard_map/scatter-add | solution.py:59
  156.1 7.8 %convert_subtract_fusion = f32[768,2048]{1,0:T(8,128)} fusion(f32[768,2048]{1,0:T(8,128)} %scatter_custom_fusion, bf16[768,2048]{1,0:T(8,128)(2,1)} %param.9), kind=kLoop, calls=%fused_computation.4 | loop fusion | flops 3145728 | bytes 15728640 | tf_op jit(solution)/shard_map/sub | solution.py:61
  163.9 4.6 %gather_fusion.1 = f32[64,2048]{1,0:T(8,128)} fusion(f32[768,2048]{1,0:T(8,128)} %convert_subtract_fusion, s32[1024]{0:T(1024)S(1)} %pad_clamp_fusion), kind=kCustom, calls=%fused_computation.1 | custom fusion | bytes 1048832 | tf_op jit(solution)/shard_map/gather | solution.py:62
  170.4 4.2 %all-to-all-start.2 = ((bf16[4,16,2048]{2,1,0:T(8,128)(2,1)}), bf16[4,16,2048]{2,1,0:T(8,128)(2,1)}, u32[]{:S(2)}, u32[]{:S(2)}) async-start(bf16[4,16,2048]{2,1,0:T(8,128)(2,1)} %multiply_convert_fusion), calls=%async_computation.2 | async-start | bytes 524288 | tf_op jit(solution)/shard_map/all_to_all | solution.py:19
  174.6 5.8 %all-to-all-done.2 = bf16[4,16,2048]{2,1,0:T(8,128)(2,1)} async-done(((bf16[4,16,2048]{2,1,0:T(8,128)(2,1)}), bf16[4,16,2048]{2,1,0:T(8,128)(2,1)}, u32[]{:S(2)}, u32[]{:S(2)}) %all-to-all-start.2) | async-done | bytes 262176 | tf_op jit(solution)/shard_map/all_to_all | solution.py:19
  184.6 4.8 %collective-permute-done = bf16[1,64,768]{2,1,0:T(8,128)(2,1)} collective-permute-done((bf16[1,64,768]{2,1,0:T(8,128)(2,1)S(1)}, bf16[1,64,768]{2,1,0:T(8,128)(2,1)}, u32[]{:S(2)}, u32[]{:S(2)}) %collective-permute-start) | collective-permute-done | bytes 98336 | tf_op jit(solution)/shard_map/ppermute | solution.py:12
  191.6 3.7 %reduce.9 = bf16[64,2048]{1,0:T(8,128)(2,1)} reduce(bf16[64,1,2048]{2,1,0:T(2,128)(2,1)} %bitcast.129, bf16[]{:T(256)} %broadcast.135), dimensions={1}, to_apply=%bitcast.113.reduce_sub_computation | reduce | bytes 524290
  197.2 4.0 %all-to-all-start.3 = ((bf16[4,2,16384]{2,1,0:T(2,128)(2,1)}), bf16[4,2,16384]{2,1,0:T(2,128)(2,1)}, u32[]{:S(2)}, u32[]{:S(2)}) async-start(bf16[4,2,16384]{2,1,0:T(2,128)(2,1)} %reshape.297), calls=%async_computation.3 | async-start | bytes 524288 | tf_op jit(solution)/shard_map/all_to_all | solution.py:23
  201.3 17.6 %all-gather.1 = bf16[512,768]{1,0:T(8,128)(2,1)} all-gather(bf16[64,768]{1,0:T(8,128)(2,1)} %copy-done.5), channel_id=3, replica_groups=mesh['dp'=8,'expert'=4] {'dp'}, dimensions={0}, use_global_device_ids=true | all-gather | bytes 884736 | tf_op jit(solution)/shard_map/all_gather | solution.py:87
  218.9 3.4 %copy.43 = bf16[1,64,2048]{1,0,2:T(2,128)(2,1)} copy(bf16[1,64,2048]{2,1,0:T(8,128)(2,1)} %bitcast.24) | data formatting | bytes 524288 | tf_op jit(solution)/shard_map/all_to_all | solution.py:19
  222.3 13.3 %reduce.11 = bf16[2048,64]{1,0:T(8,128)(2,1)} reduce(bf16[2048,1,64]{2,1,0:T(2,128)(2,1)} %bitcast.120, bf16[]{:T(256)} %broadcast.135), dimensions={1}, to_apply=%bitcast.94.reduce_sub_computation | reduce | bytes 524290
  238.0 4.7 %all-to-all-start.5 = ((bf16[8,2,8192]{2,1,0:T(2,128)(2,1)}), bf16[8,2,8192]{2,1,0:T(2,128)(2,1)}, u32[]{:S(2)}, u32[]{:S(2)}) async-start(bf16[8,2,8192]{2,1,0:T(2,128)(2,1)} %reshape.301), calls=%async_computation.5 | async-start | bytes 524288 | tf_op jit(solution)/shard_map/all_to_all | solution.py:85
  242.8 20.0 %all-gather = bf16[512,768]{1,0:T(8,128)(2,1)S(1)} all-gather(bf16[64,768]{1,0:T(8,128)(2,1)} %copy-done.6), channel_id=2, replica_groups=mesh['dp'=8,'expert'=4] {'dp'}, dimensions={0}, use_global_device_ids=true | all-gather | bytes 884736 | tf_op jit(solution)/shard_map/all_gather | solution.py:88
  269.3 5.1 %scatter_custom_fusion.1 = f32[768,2048]{1,0:T(8,128)} fusion(s32[64]{0:T(128)S(1)} %fusion.43, f32[]{:T(128)} %constant.15.clone.1, bf16[1,64,2048]{2,0,1:T(2,128)(2,1)} %bitcast.130), kind=kCustom, calls=%fused_computation.17 | custom fusion | flops 262144 | bytes 6553604 | tf_op jit(solution)/shard_map/scatter-add | solution.py:79
  274.4 4.9 %convert_element_type.75 = bf16[768,2048]{1,0:T(8,128)(2,1)} convert(f32[768,2048]{1,0:T(8,128)} %scatter_custom_fusion.1) | non-fusion elementwise | flops 1572864 | bytes 9437184 | tf_op jit(solution)/shard_map/convert_element_type | solution.py:80
  287.4 6.1 %collective-permute-done.5 = bf16[1,64,768]{2,1,0:T(8,128)(2,1)} collective-permute-done((bf16[1,64,768]{2,1,0:T(8,128)(2,1)}, bf16[1,64,768]{2,1,0:T(8,128)(2,1)}, u32[]{:S(2)}, u32[]{:S(2)}) %collective-permute-start.5) | collective-permute-done | bytes 98336 | tf_op jit(solution)/shard_map/ppermute | solution.py:12
  (108 shorter events, 85.3 us)
Async XLA Ops:
  7.2 43.4 %all-gather.6.cloned.1.call-start = ((), (), s32[]{:S(2)}) async-start(), calls=%async_computation.6 | async-start | bytes 3538944 | tf_op jit(solution)/shard_map/all_gather | solution.py:40
  7.9 3.0 copy-start.9
  7.9 83.1 %all-gather.8.cloned.1.call-start = ((), (), s32[]{:S(2)}) async-start(), calls=%async_computation.7 | async-start | bytes 3538944 | tf_op jit(solution)/shard_map/all_gather | solution.py:41
  8.7 121.2 %all-gather.10.cloned.1.call-start = ((), (), s32[]{:S(2)}) async-start(), calls=%async_computation.8 | async-start | bytes 3538944 | tf_op jit(solution)/shard_map/all_gather | solution.py:42
  10.2 7.3 %copy-start.7 = (s32[1,4,1,16]{3,2,1,0:T(1,128)S(1)}, s32[1,4,1,16]{3,2,1,0:T(1,128)}, u32[]{:S(2)}) copy-start(s32[1,4,1,16]{3,2,1,0:T(1,128)} %param.10) | copy-start | bytes 772
  10.2 8.7 %copy-start.8 = (f32[1,4,1,16]{3,2,1,0:T(1,128)S(1)}, f32[1,4,1,16]{3,2,1,0:T(1,128)}, u32[]{:S(2)}) copy-start(f32[1,4,1,16]{3,2,1,0:T(1,128)} %param.12) | copy-start | bytes 772
  11.8 10.6 %all-to-all-start = ((bf16[4,16,2048]{2,1,0:T(8,128)(2,1)}), bf16[4,16,2048]{2,1,0:T(8,128)(2,1)S(1)}, u32[]{:S(2)}, u32[]{:S(2)}) async-start(bf16[4,16,2048]{2,1,0:T(8,128)(2,1)} %broadcast_multiply_fusion), calls=%async_computation | async-start | bytes 524288 | tf_op jit(solution)/shard_map/all_to_all | solution.py:19
  40.2 97.7 %all-to-all-start.4 = ((bf16[8,2,8192]{2,1,0:T(2,128)(2,1)}), bf16[8,2,8192]{2,1,0:T(2,128)(2,1)}, u32[]{:S(2)}, u32[]{:S(2)}) async-start(bf16[8,2,8192]{2,1,0:T(2,128)(2,1)} %reshape.299), calls=%async_computation.4 | async-start | bytes 524288 | tf_op jit(solution)/shard_map/all_to_all | solution.py:84
  94.2 38.6 %copy-start.5 = (bf16[64,768]{1,0:T(8,128)(2,1)}, bf16[64,768]{1,0:T(8,128)(2,1)S(1)}, u32[]{:S(2)}) copy-start(bf16[64,768]{1,0:T(8,128)(2,1)S(1)} %get-tuple-element.28) | copy-start | bytes 294916
  137.9 12.1 %all-to-all-start.1 = ((bf16[4,2,16384]{2,1,0:T(2,128)(2,1)}), bf16[4,2,16384]{2,1,0:T(2,128)(2,1)S(1)}, u32[]{:S(2)}, u32[]{:S(2)}) async-start(bf16[4,2,16384]{2,1,0:T(2,128)(2,1)} %reshape.295), calls=%async_computation.1 | async-start | bytes 524288 | tf_op jit(solution)/shard_map/all_to_all | solution.py:23
  163.9 10.6 %copy-start.4 = (bf16[8,8,8,256]{3,2,1,0:T(8,128)(2,1)S(1)}, bf16[8,8,8,256]{3,2,1,0:T(8,128)(2,1)}, u32[]{:S(2)}) copy-start(bf16[8,8,8,256]{3,2,1,0:T(8,128)(2,1)} %copy.49) | copy-start | bytes 786436
  170.4 10.1 %all-to-all-start.2 = ((bf16[4,16,2048]{2,1,0:T(8,128)(2,1)}), bf16[4,16,2048]{2,1,0:T(8,128)(2,1)}, u32[]{:S(2)}, u32[]{:S(2)}) async-start(bf16[4,16,2048]{2,1,0:T(8,128)(2,1)} %multiply_convert_fusion), calls=%async_computation.2 | async-start | bytes 524288 | tf_op jit(solution)/shard_map/all_to_all | solution.py:19
  183.3 6.0 %copy-start.6 = (bf16[64,768]{1,0:T(8,128)(2,1)}, bf16[64,768]{1,0:T(8,128)(2,1)S(1)}, u32[]{:S(2)}) copy-start(bf16[64,768]{1,0:T(8,128)(2,1)S(1)} %get-tuple-element.24) | copy-start | bytes 294916
  183.3 6.0 %copy-start.1 = (bf16[2048,1,768]{2,0,1:T(8,128)(2,1)S(1)}, bf16[2048,1,768]{2,0,1:T(8,128)(2,1)}, u32[]{:S(2)}) copy-start(bf16[2048,1,768]{2,0,1:T(8,128)(2,1)} %all-gather.6.cloned.1.call-done) | copy-start | bytes 9437188
  183.3 6.0 %collective-permute-start = (bf16[1,64,768]{2,1,0:T(8,128)(2,1)S(1)}, bf16[1,64,768]{2,1,0:T(8,128)(2,1)}, u32[]{:S(2)}, u32[]{:S(2)}) collective-permute-start(bf16[1,64,768]{2,1,0:T(8,128)(2,1)S(1)} %bitcast.131), channel_id=1, source_target_pairs={{0,4},{4,8},{8,12},{12,16},{16,20},{20,24},{24,28},{28,0},{1,5},{5... | collective-permute-start | bytes 294920 | tf_op jit(solution)/shard_map/ppermute | solution.py:12
  189.3 11.9 %collective-permute-start.1 = (bf16[1,64,768]{2,1,0:T(8,128)(2,1)}, bf16[1,64,768]{2,1,0:T(8,128)(2,1)}, u32[]{:S(2)}, u32[]{:S(2)}) collective-permute-start(bf16[1,64,768]{2,1,0:T(8,128)(2,1)} %collective-permute-done), channel_id=1, source_target_pairs={{0,4},{4,8},{8,12},{12,16},{16,20},{20,24},{24,28},{28,0},{1,5},{5... | collective-permute-start | bytes 294920 | tf_op jit(solution)/shard_map/ppermute | solution.py:12
  197.2 40.9 %all-to-all-start.3 = ((bf16[4,2,16384]{2,1,0:T(2,128)(2,1)}), bf16[4,2,16384]{2,1,0:T(2,128)(2,1)}, u32[]{:S(2)}, u32[]{:S(2)}) async-start(bf16[4,2,16384]{2,1,0:T(2,128)(2,1)} %reshape.297), calls=%async_computation.3 | async-start | bytes 524288 | tf_op jit(solution)/shard_map/all_to_all | solution.py:23
  201.2 36.5 %collective-permute-start.2 = (bf16[1,64,768]{2,1,0:T(8,128)(2,1)}, bf16[1,64,768]{2,1,0:T(8,128)(2,1)}, u32[]{:S(2)}, u32[]{:S(2)}) collective-permute-start(bf16[1,64,768]{2,1,0:T(8,128)(2,1)} %collective-permute-done.1), channel_id=1, source_target_pairs={{0,4},{4,8},{8,12},{12,16},{16,20},{20,24},{24,28},{28,0},{1,5},{5... | collective-permute-start | bytes 294920 | tf_op jit(solution)/shard_map/ppermute | solution.py:12
  237.7 25.1 %collective-permute-start.3 = (bf16[1,64,768]{2,1,0:T(8,128)(2,1)}, bf16[1,64,768]{2,1,0:T(8,128)(2,1)}, u32[]{:S(2)}, u32[]{:S(2)}) collective-permute-start(bf16[1,64,768]{2,1,0:T(8,128)(2,1)} %collective-permute-done.2), channel_id=1, source_target_pairs={{0,4},{4,8},{8,12},{12,16},{16,20},{20,24},{24,28},{28,0},{1,5},{5... | collective-permute-start | bytes 294920 | tf_op jit(solution)/shard_map/ppermute | solution.py:12
  238.0 41.3 %all-to-all-start.5 = ((bf16[8,2,8192]{2,1,0:T(2,128)(2,1)}), bf16[8,2,8192]{2,1,0:T(2,128)(2,1)}, u32[]{:S(2)}, u32[]{:S(2)}) async-start(bf16[8,2,8192]{2,1,0:T(2,128)(2,1)} %reshape.301), calls=%async_computation.5 | async-start | bytes 524288 | tf_op jit(solution)/shard_map/all_to_all | solution.py:85
  262.8 24.4 %collective-permute-start.4 = (bf16[1,64,768]{2,1,0:T(8,128)(2,1)}, bf16[1,64,768]{2,1,0:T(8,128)(2,1)}, u32[]{:S(2)}, u32[]{:S(2)}) collective-permute-start(bf16[1,64,768]{2,1,0:T(8,128)(2,1)} %collective-permute-done.3), channel_id=1, source_target_pairs={{0,4},{4,8},{8,12},{12,16},{16,20},{20,24},{24,28},{28,0},{1,5},{5... | collective-permute-start | bytes 294920 | tf_op jit(solution)/shard_map/ppermute | solution.py:12
  286.1 7.3 %copy-start.3 = (bf16[512,768]{1,0:T(8,128)(2,1)S(1)}, bf16[512,768]{1,0:T(8,128)(2,1)}, u32[]{:S(2)}) copy-start(bf16[512,768]{1,0:T(8,128)(2,1)} %all-gather.1) | copy-start | bytes 2359300
  287.2 6.2 %collective-permute-start.5 = (bf16[1,64,768]{2,1,0:T(8,128)(2,1)}, bf16[1,64,768]{2,1,0:T(8,128)(2,1)}, u32[]{:S(2)}, u32[]{:S(2)}) collective-permute-start(bf16[1,64,768]{2,1,0:T(8,128)(2,1)} %collective-permute-done.4), channel_id=1, source_target_pairs={{0,4},{4,8},{8,12},{12,16},{16,20},{20,24},{24,28},{28,0},{1,5},{5... | collective-permute-start | bytes 294920 | tf_op jit(solution)/shard_map/ppermute | solution.py:12
  293.4 6.2 %collective-permute-start.6 = (bf16[1,64,768]{2,1,0:T(8,128)(2,1)}, bf16[1,64,768]{2,1,0:T(8,128)(2,1)}, u32[]{:S(2)}, u32[]{:S(2)}) collective-permute-start(bf16[1,64,768]{2,1,0:T(8,128)(2,1)} %collective-permute-done.5), channel_id=1, source_target_pairs={{0,4},{4,8},{8,12},{12,16},{16,20},{20,24},{24,28},{28,0},{1,5},{5... | collective-permute-start | bytes 294920 | tf_op jit(solution)/shard_map/ppermute | solution.py:12
  (2 other events, 6.1 us)
Sparse Core Ops, SparseCore 0:
  9.6 40.9 all-gather.5
  52.2 38.7 all-gather.7
  92.7 37.1 all-gather.9
